TPU v7x, 128 devices: a whole 4x4x4 slice. The times are simulated.
128 devices in a mesh: sx: 8 (over y_hi, x), sy: 8 (over z, core), par: 2 (over y_lo).
Axes of the slice: x: 4, y: 4 (y_hi: 2, y_lo: 2; y = y_hi * 2 + y_lo), z: 4, core: 2. Of those that a mesh axis runs over, the one named last changes fastest.
Arguments:
- initial_state: float32 [64, 128, 128, 128], P('par', 'sx', 'sy'), may hold values from -6 to 6
- conductivity: float32 [64, 128, 128, 128], P('par', 'sx', 'sy'), may hold values from 0.1 to 1
- omega: bfloat16 [64, 64], replicated, may hold values from -0.75 to 0.75
- psi: bfloat16 [64, 128, 128, 128], P(None, 'sx', 'sy'), may hold values from -0.01171875 to 0.01171875
- range_prev: bfloat16 [64, 128, 128, 128], P('par', 'sx', 'sy'), may hold values from -3 to 3
- corange_prev: float32 [64, 64], P(None, 'par'), may hold values from -3 to 3
Outputs:
- final_state: float32 [64, 128, 128, 128], P('par', 'sx', 'sy')
- range_sketch: bfloat16 [64, 128, 128, 128], P('par', 'sx', 'sy')
- corange_sketch: float32 [64, 64], P(None, 'par')
All inputs are finite; a program needn't handle non-finite values.
Results may differ from a plain program's by a relative error of at most 0.0033.
Values may be sent and summed in bfloat16 or wider, within the bound.
A program may use at most 192 MiB of HBM per device.

v0:
```python
import jax
import jax.numpy as jnp
from jax import lax
from jax.sharding import PartitionSpec as P

STEPS = 4


def extended(block, sides, width):
    for axis, dim in sides:
        count = lax.axis_size(axis)
        forward = [(i, i + 1) for i in range(count - 1)]
        backward = [(target, source) for source, target in forward]
        low = lax.ppermute(
            lax.slice_in_dim(block, block.shape[dim] - width, None, axis=dim), axis, forward
        )
        high = lax.ppermute(lax.slice_in_dim(block, 0, width, axis=dim), axis, backward)
        block = jnp.concatenate([low, block, high], axis=dim)
    return block


def advance(field, kpad):
    center = field[:, 1:-1, 1:-1, :]
    kcen = kpad[:, 1:-1, 1:-1, :]
    width_x = center.shape[1]
    width_y = center.shape[2]
    zfield = jnp.pad(center, ((0, 0), (0, 0), (0, 0), (1, 1)))
    zcond = jnp.pad(kcen, ((0, 0), (0, 0), (0, 0), (1, 1)))
    length = center.shape[3]
    pairs = [
        (field[:, 2:, 1:-1, :], kpad[:, 2:, 1:-1, :]),
        (field[:, :width_x, 1:-1, :], kpad[:, :width_x, 1:-1, :]),
        (field[:, 1:-1, 2:, :], kpad[:, 1:-1, 2:, :]),
        (field[:, 1:-1, :width_y, :], kpad[:, 1:-1, :width_y, :]),
        (zfield[:, :, :, 2:], zcond[:, :, :, 2:]),
        (zfield[:, :, :, :length], zcond[:, :, :, :length]),
    ]
    total = jnp.zeros_like(center)
    for unb, knb in pairs:
        total = total + 0.5 * (kcen + knb) * (unb - center)
    return center + 0.16 * total


def per_device(initial_state, conductivity, omega, psi, range_prev, corange_prev):
    samples, cells_x, cells_y, length = initial_state.shape
    kpad = extended(conductivity, (("sx", 1), ("sy", 2)), 1)
    state = initial_state
    for step in range(STEPS):
        field = extended(state, (("sx", 1), ("sy", 2)), 1)
        state = advance(field, kpad)
    snapshot = state.astype(jnp.bfloat16)
    flat_snap = snapshot.reshape(samples, cells_x * cells_y * length)
    rank = omega.shape[1]
    rank_dev = range_prev.shape[0]
    own_cols = lax.dynamic_slice_in_dim(omega, lax.axis_index("par") * rank_dev, rank_dev, 1)
    start_sum = range_prev.astype(jnp.float32)
    piece = lax.all_gather(snapshot, "par", axis=0, tiled=True)
    rows = piece.shape[0]
    term = lax.dot_general(
        own_cols,
        piece.reshape(rows, -1),
        (((0,), (0,)), ((), ())),
        preferred_element_type=jnp.float32,
    )
    range_sum = start_sum + term.reshape(start_sum.shape)
    range_sketch = range_sum.astype(jnp.bfloat16)
    flat_psi = psi.reshape(rank, cells_x * cells_y * length)
    partial_value = lax.dot_general(
        flat_psi, flat_snap, (((1,), (1,)), ((), ())), preferred_element_type=jnp.float32
    )
    corange_sketch = corange_prev + lax.psum(partial_value, ("sx", "sy"))
    return (state, range_sketch, corange_sketch)


def solution(mesh):
    in_specs = (
        P("par", "sx", "sy", None),
        P("par", "sx", "sy", None),
        P(),
        P(None, "sx", "sy", None),
        P("par", "sx", "sy", None),
        P(None, "par"),
    )
    out_specs = (P("par", "sx", "sy", None), P("par", "sx", "sy", None), P(None, "par"))
    return jax.shard_map(
        per_device, mesh=mesh, in_specs=in_specs, out_specs=out_specs, check_vma=False
    )
```

profile of v0, /device:TPU:24, one launch (start us, length us, event | category | flops | bytes accessed | tf_op | source)
XLA Modules:
  0.0 525.8 jit_solution(14510973290693297946)
XLA Ops:
  7.2 4.8 copy.22
  12.0 3.4 collective-permute-start.2
  15.5 6.3 %collective-permute-start = (f32[32,1,16,128]{3,0,2,1:T(8,128)S(1)}, f32[32,1,16,128]{3,0,2,1:T(8,128)S(1)}, u32[]{:S(2)}, u32[]{:S(2)}) collective-permute-start(f32[32,1,16,128]{3,0,2,1:T(8,128)S(1)} %get-tuple-element.31), channel_id=1, source_target_pairs={{16,0},{32,16},{48,32},{64,48},{80,64},{96,80},{112,96},{17,1},{33... | collective-permute-start | bytes 786440 | tf_op jit(solution)/shard_map/ppermute | solution.py:17
  26.2 7.5 %collective-permute-start.1 = (f32[32,1,16,128]{3,0,2,1:T(8,128)S(1)}, f32[32,1,16,128]{3,0,2,1:T(8,128)S(1)}, u32[]{:S(2)}, u32[]{:S(2)}) collective-permute-start(f32[32,1,16,128]{3,0,2,1:T(8,128)S(1)} %get-tuple-element.32), channel_id=1, source_target_pairs={{16,0},{32,16},{48,32},{64,48},{80,64},{96,80},{112,96},{17,1},{33... | collective-permute-start | bytes 786440 | tf_op jit(solution)/shard_map/ppermute | solution.py:17
  41.4 4.4 constant_dynamic-update-slice_fusion.4
  48.9 4.3 collective-permute-start.7
  54.2 10.3 %fusion.9 = f32[32,16,16,128]{3,0,2,1:T(8,128)S(1)} fusion(f32[32,16,16,128]{3,0,2,1:T(8,128)S(1)} %copy.44, f32[32,18,16,128]{3,0,2,1:T(8,128)} %constant_dynamic-update-slice_fusion.3, f32[32,18,1,128]{3,0,2,1:T(8,128)S(1)} %collective-permute-done.7, f32[32,18,1,128]{3,0,2,1:T(8,128)S(1)} %collective-permute-done.5, ...), kind=kLoop, calls=%fused_computation.19 | loop fusion | flops 40894464 | bytes 24248320 | tf_op jit(solution)/shard_map/add | solution.py:41
  66.5 3.9 collective-permute-start.9
  72.8 5.5 %collective-permute-done.9 = f32[32,1,16,128]{3,0,2,1:T(8,128)S(1)} collective-permute-done((f32[32,1,16,128]{3,0,2,1:T(8,128)S(1)}, f32[32,1,16,128]{3,0,2,1:T(8,128)S(1)}, u32[]{:S(2)}, u32[]{:S(2)}) %collective-permute-start.9) | collective-permute-done | bytes 262176 | tf_op jit(solution)/shard_map/ppermute | solution.py:14
  79.7 5.6 %collective-permute-start.11 = (f32[32,18,1,128]{3,0,2,1:T(8,128)S(1)}, f32[32,18,1,128]{3,0,2,1:T(8,128)S(1)}, u32[]{:S(2)}, u32[]{:S(2)}) collective-permute-start(f32[32,18,1,128]{3,0,2,1:T(8,128)S(1)} %get-tuple-element.19), channel_id=1, source_target_pairs={{0,2},{2,4},{4,6},{6,8},{8,10},{10,12},{12,14},{1,3},{3,5},{5,7},{... | collective-permute-start | bytes 884744 | tf_op jit(solution)/shard_map/ppermute | solution.py:14
  86.5 8.1 %fusion.17 = f32[32,16,16,128]{3,0,2,1:T(8,128)S(1)} fusion(f32[32,16,16,128]{3,0,2,1:T(8,128)S(1)} %fusion.9, f32[32,18,1,128]{3,0,2,1:T(8,128)S(1)} %collective-permute-done.11, f32[32,1,16,128]{3,0,2,1:T(8,128)S(1)} %collective-permute-done.8, f32[32,1,16,128]{3,0,2,1:T(8,128)S(1)} %collective-permute-done.9, ...), kind=kLoop, calls=%fused_computation.27 | loop fusion | flops 45088768 | bytes 19529728 | tf_op jit(solution)/shard_map/add | solution.py:41
  96.5 3.9 collective-permute-start.13
  102.9 5.5 %collective-permute-done.13 = f32[32,1,16,128]{3,0,2,1:T(8,128)S(1)} collective-permute-done((f32[32,1,16,128]{3,0,2,1:T(8,128)S(1)}, f32[32,1,16,128]{3,0,2,1:T(8,128)S(1)}, u32[]{:S(2)}, u32[]{:S(2)}) %collective-permute-start.13) | collective-permute-done | bytes 262176 | tf_op jit(solution)/shard_map/ppermute | solution.py:14
  109.8 8.9 %collective-permute-start.15 = (f32[32,18,1,128]{3,0,2,1:T(8,128)S(1)}, f32[32,18,1,128]{3,0,2,1:T(8,128)S(1)}, u32[]{:S(2)}, u32[]{:S(2)}) collective-permute-start(f32[32,18,1,128]{3,0,2,1:T(8,128)S(1)} %get-tuple-element.17), channel_id=1, source_target_pairs={{0,2},{2,4},{4,6},{6,8},{8,10},{10,12},{12,14},{1,3},{3,5},{5,7},{... | collective-permute-start | bytes 884744 | tf_op jit(solution)/shard_map/ppermute | solution.py:14
  119.8 8.1 %fusion.25 = f32[32,16,16,128]{3,0,2,1:T(8,128)S(1)} fusion(f32[32,16,16,128]{3,0,2,1:T(8,128)S(1)} %fusion.17, f32[32,18,1,128]{3,0,2,1:T(8,128)S(1)} %collective-permute-done.15, f32[32,1,16,128]{3,0,2,1:T(8,128)S(1)} %collective-permute-done.12, f32[32,1,16,128]{3,0,2,1:T(8,128)S(1)} %collective-permute-done.13, ...), kind=kLoop, calls=%fused_computation.35 | loop fusion | flops 45088768 | bytes 19529728 | tf_op jit(solution)/shard_map/add | solution.py:41
  129.9 3.9 collective-permute-start.17
  136.2 5.5 %collective-permute-done.17 = f32[32,1,16,128]{3,0,2,1:T(8,128)S(1)} collective-permute-done((f32[32,1,16,128]{3,0,2,1:T(8,128)S(1)}, f32[32,1,16,128]{3,0,2,1:T(8,128)S(1)}, u32[]{:S(2)}, u32[]{:S(2)}) %collective-permute-start.17) | collective-permute-done | bytes 262176 | tf_op jit(solution)/shard_map/ppermute | solution.py:14
  143.1 8.6 %collective-permute-start.19 = (f32[32,18,1,128]{3,0,2,1:T(8,128)S(1)}, f32[32,18,1,128]{3,0,2,1:T(8,128)S(1)}, u32[]{:S(2)}, u32[]{:S(2)}) collective-permute-start(f32[32,18,1,128]{3,0,2,1:T(8,128)S(1)} %get-tuple-element.15), channel_id=1, source_target_pairs={{0,2},{2,4},{4,6},{6,8},{8,10},{10,12},{12,14},{1,3},{3,5},{5,7},{... | collective-permute-start | bytes 884744 | tf_op jit(solution)/shard_map/ppermute | solution.py:14
  152.9 9.7 %fusion.100 = (bf16[32,16,16,128]{3,0,2,1:T(8,128)(2,1)S(1)}, f32[32,16,16,128]{3,0,2,1:T(8,128)}) fusion(f32[32,16,16,128]{3,0,2,1:T(8,128)S(1)} %fusion.25, f32[32,16,16,128]{3,0,2,1:T(8,128)S(1)} %copy.22, f32[32,1,16,128]{3,0,2,1:T(8,128)S(1)} %collective-permute-done.16, f32[32,1,16,128]{3,0,2,1:T(8,128)S(1)} %collective-permute-done.17, ...), kind=kLoop, calls=%fused_computation.155 | loop fusion | flops 46137344 | bytes 21626880 | tf_op jit(solution)/shard_map/convert_element_type | solution.py:51
  164.8 6.8 %copy.50 = f32[32,16,16,128]{3,2,1,0:T(8,128)} copy(f32[32,16,16,128]{3,0,2,1:T(8,128)} %get-tuple-element.13) | data formatting | bytes 8388608
  171.6 3.7 fusion.94
  175.3 330.3 %psum.7 = f32[64,32]{0,1:T(8,128)S(1)} all-reduce(f32[64,32]{0,1:T(8,128)S(1)} %fusion.94), channel_id=1, replica_groups=mesh['sx'=8,'sy'=8,'par'=2] {'sx','sy'}, use_global_device_ids=true, to_apply=%region_0.1 | all-reduce | flops 2048 | bytes 16384 | tf_op jit(solution)/shard_map/psum | solution.py:71
  506.2 4.9 copy.69
  512.7 4.1 add_convert_fusion
  (62 shorter events, 43.2 us)
Async XLA Ops:
  7.2 505.2 %copy-start = (bf16[64,64]{1,0:T(8,128)(2,1)S(1)}, bf16[64,64]{1,0:T(8,128)(2,1)}, u32[]{:S(2)}) copy-start(bf16[64,64]{1,0:T(8,128)(2,1)} %param.8) | copy-start | bytes 24580
  7.2 499.1 %all-gather.2.cloned.1.call-start = ((), (), s32[]{:S(2)}) async-start(), calls=%async_computation | async-start | bytes 6291456 | tf_op jit(solution)/shard_map/all_gather | solution.py:57
  12.0 21.7 %collective-permute-start.2 = (f32[32,1,16,128]{3,0,2,1:T(8,128)S(1)}, f32[32,1,16,128]{3,0,2,1:T(8,128)S(1)}, u32[]{:S(2)}, u32[]{:S(2)}) collective-permute-start(f32[32,1,16,128]{3,0,2,1:T(8,128)S(1)} %get-tuple-element.30), channel_id=1, source_target_pairs={{0,16},{16,32},{32,48},{48,64},{64,80},{80,96},{96,112},{1,17},{17... | collective-permute-start | bytes 786440 | tf_op jit(solution)/shard_map/ppermute | solution.py:14
  15.5 18.3 %copy-start.1 = (f32[32,16,16,128]{3,2,1,0:T(8,128)S(1)}, f32[32,16,16,128]{3,2,1,0:T(8,128)}, u32[]{:S(2)}) copy-start(f32[32,16,16,128]{3,2,1,0:T(8,128)} %param.7) | copy-start | bytes 12582916
  15.5 20.8 %collective-permute-start = (f32[32,1,16,128]{3,0,2,1:T(8,128)S(1)}, f32[32,1,16,128]{3,0,2,1:T(8,128)S(1)}, u32[]{:S(2)}, u32[]{:S(2)}) collective-permute-start(f32[32,1,16,128]{3,0,2,1:T(8,128)S(1)} %get-tuple-element.31), channel_id=1, source_target_pairs={{16,0},{32,16},{48,32},{64,48},{80,64},{96,80},{112,96},{17,1},{33... | collective-permute-start | bytes 786440 | tf_op jit(solution)/shard_map/ppermute | solution.py:17
  24.3 16.4 %collective-permute-start.3 = (f32[32,1,16,128]{3,0,2,1:T(8,128)S(1)}, f32[32,1,16,128]{3,0,2,1:T(8,128)S(1)}, u32[]{:S(2)}, u32[]{:S(2)}) collective-permute-start(f32[32,1,16,128]{3,0,2,1:T(8,128)S(1)} %get-tuple-element.33), channel_id=1, source_target_pairs={{0,16},{16,32},{32,48},{48,64},{64,80},{80,96},{96,112},{1,17},{17... | collective-permute-start | bytes 786440 | tf_op jit(solution)/shard_map/ppermute | solution.py:14
  26.2 19.6 %collective-permute-start.1 = (f32[32,1,16,128]{3,0,2,1:T(8,128)S(1)}, f32[32,1,16,128]{3,0,2,1:T(8,128)S(1)}, u32[]{:S(2)}, u32[]{:S(2)}) collective-permute-start(f32[32,1,16,128]{3,0,2,1:T(8,128)S(1)} %get-tuple-element.32), channel_id=1, source_target_pairs={{16,0},{32,16},{48,32},{64,48},{80,64},{96,80},{112,96},{17,1},{33... | collective-permute-start | bytes 786440 | tf_op jit(solution)/shard_map/ppermute | solution.py:17
  36.3 16.9 %collective-permute-start.4 = (f32[32,18,1,128]{3,0,2,1:T(8,128)S(1)}, f32[32,18,1,128]{3,0,2,1:T(8,128)S(1)}, u32[]{:S(2)}, u32[]{:S(2)}) collective-permute-start(f32[32,18,1,128]{3,0,2,1:T(8,128)S(1)} %get-tuple-element.21), channel_id=1, source_target_pairs={{2,0},{4,2},{6,4},{8,6},{10,8},{12,10},{14,12},{3,1},{5,3},{7,5},{... | collective-permute-start | bytes 884744 | tf_op jit(solution)/shard_map/ppermute | solution.py:17
  37.6 15.6 %collective-permute-start.6 = (f32[32,18,1,128]{3,0,2,1:T(8,128)S(1)}, f32[32,18,1,128]{3,0,2,1:T(8,128)S(1)}, u32[]{:S(2)}, u32[]{:S(2)}) collective-permute-start(f32[32,18,1,128]{3,0,2,1:T(8,128)S(1)} %get-tuple-element.20), channel_id=1, source_target_pairs={{0,2},{2,4},{4,6},{6,8},{8,10},{10,12},{12,14},{1,3},{3,5},{5,7},{... | collective-permute-start | bytes 884744 | tf_op jit(solution)/shard_map/ppermute | solution.py:14
  47.6 5.6 %collective-permute-start.5 = (f32[32,18,1,128]{3,0,2,1:T(8,128)S(1)}, f32[32,18,1,128]{3,0,2,1:T(8,128)S(1)}, u32[]{:S(2)}, u32[]{:S(2)}) collective-permute-start(f32[32,18,1,128]{3,0,2,1:T(8,128)S(1)} %get-tuple-element.22), channel_id=1, source_target_pairs={{2,0},{4,2},{6,4},{8,6},{10,8},{12,10},{14,12},{3,1},{5,3},{7,5},{... | collective-permute-start | bytes 884744 | tf_op jit(solution)/shard_map/ppermute | solution.py:17
  48.9 5.3 collective-permute-start.7
  64.5 8.3 %collective-permute-start.8 = (f32[32,1,16,128]{3,0,2,1:T(8,128)S(1)}, f32[32,1,16,128]{3,0,2,1:T(8,128)S(1)}, u32[]{:S(2)}, u32[]{:S(2)}) collective-permute-start(f32[32,1,16,128]{3,0,2,1:T(8,128)S(1)} %get-tuple-element.29), channel_id=1, source_target_pairs={{16,0},{32,16},{48,32},{64,48},{80,64},{96,80},{112,96},{17,1},{33... | collective-permute-start | bytes 786440 | tf_op jit(solution)/shard_map/ppermute | solution.py:17
  66.5 11.9 %collective-permute-start.9 = (f32[32,1,16,128]{3,0,2,1:T(8,128)S(1)}, f32[32,1,16,128]{3,0,2,1:T(8,128)S(1)}, u32[]{:S(2)}, u32[]{:S(2)}) collective-permute-start(f32[32,1,16,128]{3,0,2,1:T(8,128)S(1)} %get-tuple-element.28), channel_id=1, source_target_pairs={{0,16},{16,32},{32,48},{48,64},{64,80},{80,96},{96,112},{1,17},{17... | collective-permute-start | bytes 786440 | tf_op jit(solution)/shard_map/ppermute | solution.py:14
  78.4 6.9 %collective-permute-start.10 = (f32[32,18,1,128]{3,0,2,1:T(8,128)S(1)}, f32[32,18,1,128]{3,0,2,1:T(8,128)S(1)}, u32[]{:S(2)}, u32[]{:S(2)}) collective-permute-start(f32[32,18,1,128]{3,0,2,1:T(8,128)S(1)} %get-tuple-element.18), channel_id=1, source_target_pairs={{2,0},{4,2},{6,4},{8,6},{10,8},{12,10},{14,12},{3,1},{5,3},{7,5},{... | collective-permute-start | bytes 884744 | tf_op jit(solution)/shard_map/ppermute | solution.py:17
  79.7 6.8 %collective-permute-start.11 = (f32[32,18,1,128]{3,0,2,1:T(8,128)S(1)}, f32[32,18,1,128]{3,0,2,1:T(8,128)S(1)}, u32[]{:S(2)}, u32[]{:S(2)}) collective-permute-start(f32[32,18,1,128]{3,0,2,1:T(8,128)S(1)} %get-tuple-element.19), channel_id=1, source_target_pairs={{0,2},{2,4},{4,6},{6,8},{8,10},{10,12},{12,14},{1,3},{3,5},{5,7},{... | collective-permute-start | bytes 884744 | tf_op jit(solution)/shard_map/ppermute | solution.py:14
  94.6 8.3 %collective-permute-start.12 = (f32[32,1,16,128]{3,0,2,1:T(8,128)S(1)}, f32[32,1,16,128]{3,0,2,1:T(8,128)S(1)}, u32[]{:S(2)}, u32[]{:S(2)}) collective-permute-start(f32[32,1,16,128]{3,0,2,1:T(8,128)S(1)} %get-tuple-element.27), channel_id=1, source_target_pairs={{16,0},{32,16},{48,32},{64,48},{80,64},{96,80},{112,96},{17,1},{33... | collective-permute-start | bytes 786440 | tf_op jit(solution)/shard_map/ppermute | solution.py:17
  96.5 11.9 %collective-permute-start.13 = (f32[32,1,16,128]{3,0,2,1:T(8,128)S(1)}, f32[32,1,16,128]{3,0,2,1:T(8,128)S(1)}, u32[]{:S(2)}, u32[]{:S(2)}) collective-permute-start(f32[32,1,16,128]{3,0,2,1:T(8,128)S(1)} %get-tuple-element.26), channel_id=1, source_target_pairs={{0,16},{16,32},{32,48},{48,64},{64,80},{80,96},{96,112},{1,17},{17... | collective-permute-start | bytes 786440 | tf_op jit(solution)/shard_map/ppermute | solution.py:14
  108.5 10.2 %collective-permute-start.14 = (f32[32,18,1,128]{3,0,2,1:T(8,128)S(1)}, f32[32,18,1,128]{3,0,2,1:T(8,128)S(1)}, u32[]{:S(2)}, u32[]{:S(2)}) collective-permute-start(f32[32,18,1,128]{3,0,2,1:T(8,128)S(1)} %get-tuple-element.16), channel_id=1, source_target_pairs={{2,0},{4,2},{6,4},{8,6},{10,8},{12,10},{14,12},{3,1},{5,3},{7,5},{... | collective-permute-start | bytes 884744 | tf_op jit(solution)/shard_map/ppermute | solution.py:17
  109.8 10.1 %collective-permute-start.15 = (f32[32,18,1,128]{3,0,2,1:T(8,128)S(1)}, f32[32,18,1,128]{3,0,2,1:T(8,128)S(1)}, u32[]{:S(2)}, u32[]{:S(2)}) collective-permute-start(f32[32,18,1,128]{3,0,2,1:T(8,128)S(1)} %get-tuple-element.17), channel_id=1, source_target_pairs={{0,2},{2,4},{4,6},{6,8},{8,10},{10,12},{12,14},{1,3},{3,5},{5,7},{... | collective-permute-start | bytes 884744 | tf_op jit(solution)/shard_map/ppermute | solution.py:14
  128.0 8.3 %collective-permute-start.16 = (f32[32,1,16,128]{3,0,2,1:T(8,128)S(1)}, f32[32,1,16,128]{3,0,2,1:T(8,128)S(1)}, u32[]{:S(2)}, u32[]{:S(2)}) collective-permute-start(f32[32,1,16,128]{3,0,2,1:T(8,128)S(1)} %get-tuple-element.25), channel_id=1, source_target_pairs={{16,0},{32,16},{48,32},{64,48},{80,64},{96,80},{112,96},{17,1},{33... | collective-permute-start | bytes 786440 | tf_op jit(solution)/shard_map/ppermute | solution.py:17
  129.9 11.9 %collective-permute-start.17 = (f32[32,1,16,128]{3,0,2,1:T(8,128)S(1)}, f32[32,1,16,128]{3,0,2,1:T(8,128)S(1)}, u32[]{:S(2)}, u32[]{:S(2)}) collective-permute-start(f32[32,1,16,128]{3,0,2,1:T(8,128)S(1)} %get-tuple-element.24), channel_id=1, source_target_pairs={{0,16},{16,32},{32,48},{48,64},{64,80},{80,96},{96,112},{1,17},{17... | collective-permute-start | bytes 786440 | tf_op jit(solution)/shard_map/ppermute | solution.py:14
  141.8 9.9 %collective-permute-start.18 = (f32[32,18,1,128]{3,0,2,1:T(8,128)S(1)}, f32[32,18,1,128]{3,0,2,1:T(8,128)S(1)}, u32[]{:S(2)}, u32[]{:S(2)}) collective-permute-start(f32[32,18,1,128]{3,0,2,1:T(8,128)S(1)} %get-tuple-element.14), channel_id=1, source_target_pairs={{2,0},{4,2},{6,4},{8,6},{10,8},{12,10},{14,12},{3,1},{5,3},{7,5},{... | collective-permute-start | bytes 884744 | tf_op jit(solution)/shard_map/ppermute | solution.py:17
  143.1 9.8 %collective-permute-start.19 = (f32[32,18,1,128]{3,0,2,1:T(8,128)S(1)}, f32[32,18,1,128]{3,0,2,1:T(8,128)S(1)}, u32[]{:S(2)}, u32[]{:S(2)}) collective-permute-start(f32[32,18,1,128]{3,0,2,1:T(8,128)S(1)} %get-tuple-element.15), channel_id=1, source_target_pairs={{0,2},{2,4},{4,6},{6,8},{8,10},{10,12},{12,14},{1,3},{3,5},{5,7},{... | collective-permute-start | bytes 884744 | tf_op jit(solution)/shard_map/ppermute | solution.py:14
  171.6 334.0 %copy-start.4 = (f32[64,32]{0,1:T(8,128)S(1)}, f32[64,32]{0,1:T(8,128)}, u32[]{:S(2)}) copy-start(f32[64,32]{0,1:T(8,128)} %param.11) | copy-start | bytes 24580
  (3 other events, 23.0 us)
Sparse Core Ops, SparseCore 0:
  164.9 63.2 all-gather.1
where the time goes:
time: 527 us; the launch traced here: 526 us
  blocking collectives  330 us (63%)
  starting transfers between devices  73.6 us (14%)
  other arithmetic  36.9 us (7%)
  local copies, waits for them, and re-layouts  34.4 us (7%)
  waiting for transfers between devices  28.3 us (5%)
  between operations  14.5 us (3%)
  matrix products  7.84 us (1%)
    psum x1, blocking collectives, per_device(): corange_sketch = corange_prev + lax.psum(partial_value, ('sx', 'sy'))  330 us
    ppermute x10, starting transfers between devices, extended(): lax.ppermute(lax.slice_in_dim(block, block.shape[dim] - width, None, axis...  47.4 us
    unnamed x22, local copies, waits for them, and re-layouts  30.2 us
    add x3, other arithmetic, advance(): return center + 0.16 * total  26.5 us
    ppermute x10, starting transfers between devices, extended(): lax.ppermute(lax.slice_in_dim(block, 0, width, axis=dim), axis, backward)  26.1 us
    ppermute x10, waiting for transfers between devices, extended(): lax.ppermute(lax.slice_in_dim(block, block.shape[dim] - width, None, axis...  21.1 us
  transfers between devices with their start and end apart: 21, of which 10 were waited for; matrix products, arithmetic and copies ran while one was open for 4% of the time, Pallas kernels for 0%

commit v1 on v0

--- a/solution.py
+++ b/solution.py
@@ -68,7 +68,7 @@
     partial_value = lax.dot_general(
         flat_psi, flat_snap, (((1,), (1,)), ((), ())), preferred_element_type=jnp.float32
     )
-    corange_sketch = corange_prev + lax.psum(partial_value, ("sx", "sy"))
+    corange_sketch = corange_prev + lax.psum(lax.psum(partial_value, "sx"), "sy")
     return (state, range_sketch, corange_sketch)
 
 

time: 527 us -> 263 us (0.50)
  blocking collectives: 330 us -> 66.6 us
    psum x1 -> x2, blocking collectives: 330 us -> 66.6 us  [the longest x1 37.4 us: per_device(): lax.psum(partial_value, 'sx')]
  transfers between devices with their start and end apart: 21 -> 21, of which waited for: 10 -> 10; matrix products, arithmetic and copies ran while one was open for 4% -> 9% of each run, Pallas kernels for 0% -> 0%
where the time goes in v1:
time: 263 us; the launch traced here: 262 us
  starting transfers between devices  73.6 us (28%)
  blocking collectives  66.6 us (25%)
  other arithmetic  36.9 us (14%)
  local copies, waits for them, and re-layouts  34.3 us (13%)
  waiting for transfers between devices  28.3 us (11%)
  between operations  14.5 us (6%)
  matrix products  7.84 us (3%)
    ppermute x10, starting transfers between devices, extended(): lax.ppermute(lax.slice_in_dim(block, block.shape[dim] - width, None, axis...  47.4 us
    psum x1, blocking collectives, per_device(): lax.psum(partial_value, 'sx')  37.4 us
    unnamed x22, local copies, waits for them, and re-layouts  30.2 us
    psum x1, blocking collectives, per_device(): lax.psum(lax.psum(partial_value, 'sx'), 'sy')  29.2 us
    add x3, other arithmetic, advance(): return center + 0.16 * total  26.4 us
    ppermute x10, starting transfers between devices, extended(): lax.ppermute(lax.slice_in_dim(block, 0, width, axis=dim), axis, backward)  26.1 us
    ppermute x10, waiting for transfers between devices, extended(): lax.ppermute(lax.slice_in_dim(block, block.shape[dim] - width, None, axis...  21.1 us
    convert_element_type x1, other arithmetic, per_device(): snapshot = state.astype(jnp.bfloat16)  9.72 us
  transfers between devices with their start and end apart: 21, of which 10 were waited for; matrix products, arithmetic and copies ran while one was open for 9% of the time, Pallas kernels for 0%

profile of v1, /device:TPU:24, one launch (start us, length us, event | category | flops | bytes accessed | tf_op | source)
XLA Modules:
  0.0 262.1 jit_solution(15662499828480101672)
XLA Ops:
  7.2 4.8 %copy.22 = f32[32,16,16,128]{3,0,2,1:T(8,128)S(1)} copy(f32[32,16,16,128]{3,2,1,0:T(8,128)} %param.7) | data formatting | bytes 8388608 | tf_op args[1]
  15.5 6.3 %collective-permute-start = (f32[32,1,16,128]{3,0,2,1:T(8,128)S(1)}, f32[32,1,16,128]{3,0,2,1:T(8,128)S(1)}, u32[]{:S(2)}, u32[]{:S(2)}) collective-permute-start(f32[32,1,16,128]{3,0,2,1:T(8,128)S(1)} %get-tuple-element.31), channel_id=1, source_target_pairs={{16,0},{32,16},{48,32},{64,48},{80,64},{96,80},{112,96},{17,1},{33... | collective-permute-start | bytes 786440 | tf_op jit(solution)/shard_map/ppermute | solution.py:17
  26.2 7.5 %collective-permute-start.1 = (f32[32,1,16,128]{3,0,2,1:T(8,128)S(1)}, f32[32,1,16,128]{3,0,2,1:T(8,128)S(1)}, u32[]{:S(2)}, u32[]{:S(2)}) collective-permute-start(f32[32,1,16,128]{3,0,2,1:T(8,128)S(1)} %get-tuple-element.32), channel_id=1, source_target_pairs={{16,0},{32,16},{48,32},{64,48},{80,64},{96,80},{112,96},{17,1},{33... | collective-permute-start | bytes 786440 | tf_op jit(solution)/shard_map/ppermute | solution.py:17
  41.4 4.4 %constant_dynamic-update-slice_fusion.4 = f32[32,18,16,128]{3,0,2,1:T(8,128)} fusion(f32[32,18,16,128]{3,0,2,1:T(8,128)} %constant_dynamic-update-slice_fusion.5, f32[32,16,16,128]{3,2,1,0:T(8,128)S(1)} %copy-done.2), kind=kLoop, calls=%fused_computation.152 | loop fusion | bytes 8388608
  48.9 4.3 %collective-permute-start.7 = (f32[32,18,1,128]{3,0,2,1:T(8,128)S(1)}, f32[32,18,1,128]{3,0,2,1:T(8,128)S(1)}, u32[]{:S(2)}, u32[]{:S(2)}) collective-permute-start(f32[32,18,1,128]{3,0,2,1:T(8,128)S(1)} %get-tuple-element.23), channel_id=1, source_target_pairs={{0,2},{2,4},{4,6},{6,8},{8,10},{10,12},{12,14},{1,3},{3,5},{5,7},{... | collective-permute-start | bytes 884744 | tf_op jit(solution)/shard_map/ppermute | solution.py:14
  54.2 10.3 %fusion.9 = f32[32,16,16,128]{3,0,2,1:T(8,128)S(1)} fusion(f32[32,16,16,128]{3,0,2,1:T(8,128)S(1)} %copy.44, f32[32,18,16,128]{3,0,2,1:T(8,128)} %constant_dynamic-update-slice_fusion.3, f32[32,18,1,128]{3,0,2,1:T(8,128)S(1)} %collective-permute-done.7, f32[32,18,1,128]{3,0,2,1:T(8,128)S(1)} %collective-permute-done.5, ...), kind=kLoop, calls=%fused_computation.19 | loop fusion | flops 40894464 | bytes 24248320 | tf_op jit(solution)/shard_map/add | solution.py:41
  66.4 3.9 %collective-permute-start.9 = (f32[32,1,16,128]{3,0,2,1:T(8,128)S(1)}, f32[32,1,16,128]{3,0,2,1:T(8,128)S(1)}, u32[]{:S(2)}, u32[]{:S(2)}) collective-permute-start(f32[32,1,16,128]{3,0,2,1:T(8,128)S(1)} %get-tuple-element.28), channel_id=1, source_target_pairs={{0,16},{16,32},{32,48},{48,64},{64,80},{80,96},{96,112},{1,17},{17... | collective-permute-start | bytes 786440 | tf_op jit(solution)/shard_map/ppermute | solution.py:14
  72.7 5.5 %collective-permute-done.9 = f32[32,1,16,128]{3,0,2,1:T(8,128)S(1)} collective-permute-done((f32[32,1,16,128]{3,0,2,1:T(8,128)S(1)}, f32[32,1,16,128]{3,0,2,1:T(8,128)S(1)}, u32[]{:S(2)}, u32[]{:S(2)}) %collective-permute-start.9) | collective-permute-done | bytes 262176 | tf_op jit(solution)/shard_map/ppermute | solution.py:14
  79.6 5.6 %collective-permute-start.11 = (f32[32,18,1,128]{3,0,2,1:T(8,128)S(1)}, f32[32,18,1,128]{3,0,2,1:T(8,128)S(1)}, u32[]{:S(2)}, u32[]{:S(2)}) collective-permute-start(f32[32,18,1,128]{3,0,2,1:T(8,128)S(1)} %get-tuple-element.19), channel_id=1, source_target_pairs={{0,2},{2,4},{4,6},{6,8},{8,10},{10,12},{12,14},{1,3},{3,5},{5,7},{... | collective-permute-start | bytes 884744 | tf_op jit(solution)/shard_map/ppermute | solution.py:14
  86.4 8.1 %fusion.17 = f32[32,16,16,128]{3,0,2,1:T(8,128)S(1)} fusion(f32[32,16,16,128]{3,0,2,1:T(8,128)S(1)} %fusion.9, f32[32,18,1,128]{3,0,2,1:T(8,128)S(1)} %collective-permute-done.11, f32[32,1,16,128]{3,0,2,1:T(8,128)S(1)} %collective-permute-done.8, f32[32,1,16,128]{3,0,2,1:T(8,128)S(1)} %collective-permute-done.9, ...), kind=kLoop, calls=%fused_computation.27 | loop fusion | flops 45088768 | bytes 19529728 | tf_op jit(solution)/shard_map/add | solution.py:41
  96.5 3.9 %collective-permute-start.13 = (f32[32,1,16,128]{3,0,2,1:T(8,128)S(1)}, f32[32,1,16,128]{3,0,2,1:T(8,128)S(1)}, u32[]{:S(2)}, u32[]{:S(2)}) collective-permute-start(f32[32,1,16,128]{3,0,2,1:T(8,128)S(1)} %get-tuple-element.26), channel_id=1, source_target_pairs={{0,16},{16,32},{32,48},{48,64},{64,80},{80,96},{96,112},{1,17},{17... | collective-permute-start | bytes 786440 | tf_op jit(solution)/shard_map/ppermute | solution.py:14
  102.8 5.5 %collective-permute-done.13 = f32[32,1,16,128]{3,0,2,1:T(8,128)S(1)} collective-permute-done((f32[32,1,16,128]{3,0,2,1:T(8,128)S(1)}, f32[32,1,16,128]{3,0,2,1:T(8,128)S(1)}, u32[]{:S(2)}, u32[]{:S(2)}) %collective-permute-start.13) | collective-permute-done | bytes 262176 | tf_op jit(solution)/shard_map/ppermute | solution.py:14
  109.7 8.9 %collective-permute-start.15 = (f32[32,18,1,128]{3,0,2,1:T(8,128)S(1)}, f32[32,18,1,128]{3,0,2,1:T(8,128)S(1)}, u32[]{:S(2)}, u32[]{:S(2)}) collective-permute-start(f32[32,18,1,128]{3,0,2,1:T(8,128)S(1)} %get-tuple-element.17), channel_id=1, source_target_pairs={{0,2},{2,4},{4,6},{6,8},{8,10},{10,12},{12,14},{1,3},{3,5},{5,7},{... | collective-permute-start | bytes 884744 | tf_op jit(solution)/shard_map/ppermute | solution.py:14
  119.8 8.1 %fusion.25 = f32[32,16,16,128]{3,0,2,1:T(8,128)S(1)} fusion(f32[32,16,16,128]{3,0,2,1:T(8,128)S(1)} %fusion.17, f32[32,18,1,128]{3,0,2,1:T(8,128)S(1)} %collective-permute-done.15, f32[32,1,16,128]{3,0,2,1:T(8,128)S(1)} %collective-permute-done.12, f32[32,1,16,128]{3,0,2,1:T(8,128)S(1)} %collective-permute-done.13, ...), kind=kLoop, calls=%fused_computation.35 | loop fusion | flops 45088768 | bytes 19529728 | tf_op jit(solution)/shard_map/add | solution.py:41
  129.8 3.9 %collective-permute-start.17 = (f32[32,1,16,128]{3,0,2,1:T(8,128)S(1)}, f32[32,1,16,128]{3,0,2,1:T(8,128)S(1)}, u32[]{:S(2)}, u32[]{:S(2)}) collective-permute-start(f32[32,1,16,128]{3,0,2,1:T(8,128)S(1)} %get-tuple-element.24), channel_id=1, source_target_pairs={{0,16},{16,32},{32,48},{48,64},{64,80},{80,96},{96,112},{1,17},{17... | collective-permute-start | bytes 786440 | tf_op jit(solution)/shard_map/ppermute | solution.py:14
  136.2 5.5 %collective-permute-done.17 = f32[32,1,16,128]{3,0,2,1:T(8,128)S(1)} collective-permute-done((f32[32,1,16,128]{3,0,2,1:T(8,128)S(1)}, f32[32,1,16,128]{3,0,2,1:T(8,128)S(1)}, u32[]{:S(2)}, u32[]{:S(2)}) %collective-permute-start.17) | collective-permute-done | bytes 262176 | tf_op jit(solution)/shard_map/ppermute | solution.py:14
  143.1 8.6 %collective-permute-start.19 = (f32[32,18,1,128]{3,0,2,1:T(8,128)S(1)}, f32[32,18,1,128]{3,0,2,1:T(8,128)S(1)}, u32[]{:S(2)}, u32[]{:S(2)}) collective-permute-start(f32[32,18,1,128]{3,0,2,1:T(8,128)S(1)} %get-tuple-element.15), channel_id=1, source_target_pairs={{0,2},{2,4},{4,6},{6,8},{8,10},{10,12},{12,14},{1,3},{3,5},{5,7},{... | collective-permute-start | bytes 884744 | tf_op jit(solution)/shard_map/ppermute | solution.py:14
  152.8 9.7 %fusion.100 = (bf16[32,16,16,128]{3,0,2,1:T(8,128)(2,1)S(1)}, f32[32,16,16,128]{3,0,2,1:T(8,128)}) fusion(f32[32,16,16,128]{3,0,2,1:T(8,128)S(1)} %fusion.25, f32[32,16,16,128]{3,0,2,1:T(8,128)S(1)} %copy.22, f32[32,1,16,128]{3,0,2,1:T(8,128)S(1)} %collective-permute-done.16, f32[32,1,16,128]{3,0,2,1:T(8,128)S(1)} %collective-permute-done.17, ...), kind=kLoop, calls=%fused_computation.155 | loop fusion | flops 46137344 | bytes 21626880 | tf_op jit(solution)/shard_map/convert_element_type | solution.py:51
  164.7 6.8 %copy.50 = f32[32,16,16,128]{3,2,1,0:T(8,128)} copy(f32[32,16,16,128]{3,0,2,1:T(8,128)} %get-tuple-element.13) | data formatting | bytes 8388608
  171.5 3.7 %fusion.94 = f32[64,32]{0,1:T(8,128)S(1)} fusion(bf16[32,16,16,128]{3,0,2,1:T(8,128)(2,1)S(1)} %get-tuple-element.12, bf16[64,16,16,128]{3,2,1,0:T(8,128)(2,1)S(1)} %copy-done.5), kind=kOutput, calls=%fused_computation.136 | convolution fusion | flops 134217728 | bytes 6299648 | tf_op jit(solution)/shard_map/dot_general | solution.py:68
  175.3 37.4 %psum.14 = f32[64,32]{0,1:T(8,128)S(1)} all-reduce(f32[64,32]{0,1:T(8,128)S(1)} %fusion.94), channel_id=1, replica_groups=mesh['sx'=8,'sy'=8,'par'=2] {'sx'}, use_global_device_ids=true, to_apply=%region_0.1 | all-reduce | flops 2048 | bytes 16384 | tf_op jit(solution)/shard_map/psum | solution.py:71
  212.7 29.2 %psum.15 = f32[64,32]{0,1:T(8,128)S(1)} all-reduce(f32[64,32]{0,1:T(8,128)S(1)} %psum.14), channel_id=1, replica_groups=mesh['sx'=8,'sy'=8,'par'=2] {'sy'}, use_global_device_ids=true, to_apply=%region_1.2 | all-reduce | flops 2048 | bytes 16384 | tf_op jit(solution)/shard_map/psum | solution.py:71
  242.5 4.9 %copy.69 = bf16[8,8,256,128]{3,1,2,0:T(8,128)(2,1)S(1)} copy(bf16[8,8,256,128]{3,2,1,0:T(8,128)(2,1)} %bitcast.27) | data formatting | bytes 8388608
  249.0 4.1 %add_convert_fusion = bf16[32,16,16,128]{3,0,2,1:T(8,128)(2,1)S(1)} fusion(bf16[16,16,128,64]{2,1,0,3:T(8,128)(2,1)S(1)} %bitcast.26, bf16[32,16,16,128]{3,2,1,0:T(8,128)(2,1)S(1)} %copy-done.3, bf16[64,64]{1,0:T(8,128)(2,1)S(1)} %copy-done, s32[]{:T(128)S(6)} %select_n.3), kind=kOutput, calls=%fused_computation.135 | convolution fusion | flops 137363456 | bytes 8396804 | tf_op jit(solution)/shard_map/dot_general | solution.py:59
  (63 shorter events, 46.6 us)
Async XLA Ops:
  7.2 241.4 %copy-start = (bf16[64,64]{1,0:T(8,128)(2,1)S(1)}, bf16[64,64]{1,0:T(8,128)(2,1)}, u32[]{:S(2)}) copy-start(bf16[64,64]{1,0:T(8,128)(2,1)} %param.8) | copy-start | bytes 24580
  7.2 235.3 %all-gather.2.cloned.1.call-start = ((), (), s32[]{:S(2)}) async-start(), calls=%async_computation | async-start | bytes 6291456 | tf_op jit(solution)/shard_map/all_gather | solution.py:57
  12.0 21.7 %collective-permute-start.2 = (f32[32,1,16,128]{3,0,2,1:T(8,128)S(1)}, f32[32,1,16,128]{3,0,2,1:T(8,128)S(1)}, u32[]{:S(2)}, u32[]{:S(2)}) collective-permute-start(f32[32,1,16,128]{3,0,2,1:T(8,128)S(1)} %get-tuple-element.30), channel_id=1, source_target_pairs={{0,16},{16,32},{32,48},{48,64},{64,80},{80,96},{96,112},{1,17},{17... | collective-permute-start | bytes 786440 | tf_op jit(solution)/shard_map/ppermute | solution.py:14
  15.5 18.3 %copy-start.1 = (f32[32,16,16,128]{3,2,1,0:T(8,128)S(1)}, f32[32,16,16,128]{3,2,1,0:T(8,128)}, u32[]{:S(2)}) copy-start(f32[32,16,16,128]{3,2,1,0:T(8,128)} %param.7) | copy-start | bytes 12582916
  15.5 20.8 %collective-permute-start = (f32[32,1,16,128]{3,0,2,1:T(8,128)S(1)}, f32[32,1,16,128]{3,0,2,1:T(8,128)S(1)}, u32[]{:S(2)}, u32[]{:S(2)}) collective-permute-start(f32[32,1,16,128]{3,0,2,1:T(8,128)S(1)} %get-tuple-element.31), channel_id=1, source_target_pairs={{16,0},{32,16},{48,32},{64,48},{80,64},{96,80},{112,96},{17,1},{33... | collective-permute-start | bytes 786440 | tf_op jit(solution)/shard_map/ppermute | solution.py:17
  24.3 16.4 %collective-permute-start.3 = (f32[32,1,16,128]{3,0,2,1:T(8,128)S(1)}, f32[32,1,16,128]{3,0,2,1:T(8,128)S(1)}, u32[]{:S(2)}, u32[]{:S(2)}) collective-permute-start(f32[32,1,16,128]{3,0,2,1:T(8,128)S(1)} %get-tuple-element.33), channel_id=1, source_target_pairs={{0,16},{16,32},{32,48},{48,64},{64,80},{80,96},{96,112},{1,17},{17... | collective-permute-start | bytes 786440 | tf_op jit(solution)/shard_map/ppermute | solution.py:14
  26.2 19.6 %collective-permute-start.1 = (f32[32,1,16,128]{3,0,2,1:T(8,128)S(1)}, f32[32,1,16,128]{3,0,2,1:T(8,128)S(1)}, u32[]{:S(2)}, u32[]{:S(2)}) collective-permute-start(f32[32,1,16,128]{3,0,2,1:T(8,128)S(1)} %get-tuple-element.32), channel_id=1, source_target_pairs={{16,0},{32,16},{48,32},{64,48},{80,64},{96,80},{112,96},{17,1},{33... | collective-permute-start | bytes 786440 | tf_op jit(solution)/shard_map/ppermute | solution.py:17
  36.3 16.8 %collective-permute-start.4 = (f32[32,18,1,128]{3,0,2,1:T(8,128)S(1)}, f32[32,18,1,128]{3,0,2,1:T(8,128)S(1)}, u32[]{:S(2)}, u32[]{:S(2)}) collective-permute-start(f32[32,18,1,128]{3,0,2,1:T(8,128)S(1)} %get-tuple-element.21), channel_id=1, source_target_pairs={{2,0},{4,2},{6,4},{8,6},{10,8},{12,10},{14,12},{3,1},{5,3},{7,5},{... | collective-permute-start | bytes 884744 | tf_op jit(solution)/shard_map/ppermute | solution.py:17
  37.6 15.6 %collective-permute-start.6 = (f32[32,18,1,128]{3,0,2,1:T(8,128)S(1)}, f32[32,18,1,128]{3,0,2,1:T(8,128)S(1)}, u32[]{:S(2)}, u32[]{:S(2)}) collective-permute-start(f32[32,18,1,128]{3,0,2,1:T(8,128)S(1)} %get-tuple-element.20), channel_id=1, source_target_pairs={{0,2},{2,4},{4,6},{6,8},{8,10},{10,12},{12,14},{1,3},{3,5},{5,7},{... | collective-permute-start | bytes 884744 | tf_op jit(solution)/shard_map/ppermute | solution.py:14
  47.6 5.6 %collective-permute-start.5 = (f32[32,18,1,128]{3,0,2,1:T(8,128)S(1)}, f32[32,18,1,128]{3,0,2,1:T(8,128)S(1)}, u32[]{:S(2)}, u32[]{:S(2)}) collective-permute-start(f32[32,18,1,128]{3,0,2,1:T(8,128)S(1)} %get-tuple-element.22), channel_id=1, source_target_pairs={{2,0},{4,2},{6,4},{8,6},{10,8},{12,10},{14,12},{3,1},{5,3},{7,5},{... | collective-permute-start | bytes 884744 | tf_op jit(solution)/shard_map/ppermute | solution.py:17
  48.9 5.3 %collective-permute-start.7 = (f32[32,18,1,128]{3,0,2,1:T(8,128)S(1)}, f32[32,18,1,128]{3,0,2,1:T(8,128)S(1)}, u32[]{:S(2)}, u32[]{:S(2)}) collective-permute-start(f32[32,18,1,128]{3,0,2,1:T(8,128)S(1)} %get-tuple-element.23), channel_id=1, source_target_pairs={{0,2},{2,4},{4,6},{6,8},{8,10},{10,12},{12,14},{1,3},{3,5},{5,7},{... | collective-permute-start | bytes 884744 | tf_op jit(solution)/shard_map/ppermute | solution.py:14
  64.5 8.3 %collective-permute-start.8 = (f32[32,1,16,128]{3,0,2,1:T(8,128)S(1)}, f32[32,1,16,128]{3,0,2,1:T(8,128)S(1)}, u32[]{:S(2)}, u32[]{:S(2)}) collective-permute-start(f32[32,1,16,128]{3,0,2,1:T(8,128)S(1)} %get-tuple-element.29), channel_id=1, source_target_pairs={{16,0},{32,16},{48,32},{64,48},{80,64},{96,80},{112,96},{17,1},{33... | collective-permute-start | bytes 786440 | tf_op jit(solution)/shard_map/ppermute | solution.py:17
  66.4 11.9 %collective-permute-start.9 = (f32[32,1,16,128]{3,0,2,1:T(8,128)S(1)}, f32[32,1,16,128]{3,0,2,1:T(8,128)S(1)}, u32[]{:S(2)}, u32[]{:S(2)}) collective-permute-start(f32[32,1,16,128]{3,0,2,1:T(8,128)S(1)} %get-tuple-element.28), channel_id=1, source_target_pairs={{0,16},{16,32},{32,48},{48,64},{64,80},{80,96},{96,112},{1,17},{17... | collective-permute-start | bytes 786440 | tf_op jit(solution)/shard_map/ppermute | solution.py:14
  78.3 6.9 %collective-permute-start.10 = (f32[32,18,1,128]{3,0,2,1:T(8,128)S(1)}, f32[32,18,1,128]{3,0,2,1:T(8,128)S(1)}, u32[]{:S(2)}, u32[]{:S(2)}) collective-permute-start(f32[32,18,1,128]{3,0,2,1:T(8,128)S(1)} %get-tuple-element.18), channel_id=1, source_target_pairs={{2,0},{4,2},{6,4},{8,6},{10,8},{12,10},{14,12},{3,1},{5,3},{7,5},{... | collective-permute-start | bytes 884744 | tf_op jit(solution)/shard_map/ppermute | solution.py:17
  79.6 6.8 %collective-permute-start.11 = (f32[32,18,1,128]{3,0,2,1:T(8,128)S(1)}, f32[32,18,1,128]{3,0,2,1:T(8,128)S(1)}, u32[]{:S(2)}, u32[]{:S(2)}) collective-permute-start(f32[32,18,1,128]{3,0,2,1:T(8,128)S(1)} %get-tuple-element.19), channel_id=1, source_target_pairs={{0,2},{2,4},{4,6},{6,8},{8,10},{10,12},{12,14},{1,3},{3,5},{5,7},{... | collective-permute-start | bytes 884744 | tf_op jit(solution)/shard_map/ppermute | solution.py:14
  94.5 8.3 %collective-permute-start.12 = (f32[32,1,16,128]{3,0,2,1:T(8,128)S(1)}, f32[32,1,16,128]{3,0,2,1:T(8,128)S(1)}, u32[]{:S(2)}, u32[]{:S(2)}) collective-permute-start(f32[32,1,16,128]{3,0,2,1:T(8,128)S(1)} %get-tuple-element.27), channel_id=1, source_target_pairs={{16,0},{32,16},{48,32},{64,48},{80,64},{96,80},{112,96},{17,1},{33... | collective-permute-start | bytes 786440 | tf_op jit(solution)/shard_map/ppermute | solution.py:17
  96.5 11.9 %collective-permute-start.13 = (f32[32,1,16,128]{3,0,2,1:T(8,128)S(1)}, f32[32,1,16,128]{3,0,2,1:T(8,128)S(1)}, u32[]{:S(2)}, u32[]{:S(2)}) collective-permute-start(f32[32,1,16,128]{3,0,2,1:T(8,128)S(1)} %get-tuple-element.26), channel_id=1, source_target_pairs={{0,16},{16,32},{32,48},{48,64},{64,80},{80,96},{96,112},{1,17},{17... | collective-permute-start | bytes 786440 | tf_op jit(solution)/shard_map/ppermute | solution.py:14
  108.4 10.2 %collective-permute-start.14 = (f32[32,18,1,128]{3,0,2,1:T(8,128)S(1)}, f32[32,18,1,128]{3,0,2,1:T(8,128)S(1)}, u32[]{:S(2)}, u32[]{:S(2)}) collective-permute-start(f32[32,18,1,128]{3,0,2,1:T(8,128)S(1)} %get-tuple-element.16), channel_id=1, source_target_pairs={{2,0},{4,2},{6,4},{8,6},{10,8},{12,10},{14,12},{3,1},{5,3},{7,5},{... | collective-permute-start | bytes 884744 | tf_op jit(solution)/shard_map/ppermute | solution.py:17
  109.7 10.1 %collective-permute-start.15 = (f32[32,18,1,128]{3,0,2,1:T(8,128)S(1)}, f32[32,18,1,128]{3,0,2,1:T(8,128)S(1)}, u32[]{:S(2)}, u32[]{:S(2)}) collective-permute-start(f32[32,18,1,128]{3,0,2,1:T(8,128)S(1)} %get-tuple-element.17), channel_id=1, source_target_pairs={{0,2},{2,4},{4,6},{6,8},{8,10},{10,12},{12,14},{1,3},{3,5},{5,7},{... | collective-permute-start | bytes 884744 | tf_op jit(solution)/shard_map/ppermute | solution.py:14
  127.9 8.3 %collective-permute-start.16 = (f32[32,1,16,128]{3,0,2,1:T(8,128)S(1)}, f32[32,1,16,128]{3,0,2,1:T(8,128)S(1)}, u32[]{:S(2)}, u32[]{:S(2)}) collective-permute-start(f32[32,1,16,128]{3,0,2,1:T(8,128)S(1)} %get-tuple-element.25), channel_id=1, source_target_pairs={{16,0},{32,16},{48,32},{64,48},{80,64},{96,80},{112,96},{17,1},{33... | collective-permute-start | bytes 786440 | tf_op jit(solution)/shard_map/ppermute | solution.py:17
  129.8 11.9 %collective-permute-start.17 = (f32[32,1,16,128]{3,0,2,1:T(8,128)S(1)}, f32[32,1,16,128]{3,0,2,1:T(8,128)S(1)}, u32[]{:S(2)}, u32[]{:S(2)}) collective-permute-start(f32[32,1,16,128]{3,0,2,1:T(8,128)S(1)} %get-tuple-element.24), channel_id=1, source_target_pairs={{0,16},{16,32},{32,48},{48,64},{64,80},{80,96},{96,112},{1,17},{17... | collective-permute-start | bytes 786440 | tf_op jit(solution)/shard_map/ppermute | solution.py:14
  141.8 9.9 %collective-permute-start.18 = (f32[32,18,1,128]{3,0,2,1:T(8,128)S(1)}, f32[32,18,1,128]{3,0,2,1:T(8,128)S(1)}, u32[]{:S(2)}, u32[]{:S(2)}) collective-permute-start(f32[32,18,1,128]{3,0,2,1:T(8,128)S(1)} %get-tuple-element.14), channel_id=1, source_target_pairs={{2,0},{4,2},{6,4},{8,6},{10,8},{12,10},{14,12},{3,1},{5,3},{7,5},{... | collective-permute-start | bytes 884744 | tf_op jit(solution)/shard_map/ppermute | solution.py:17
  143.1 9.8 %collective-permute-start.19 = (f32[32,18,1,128]{3,0,2,1:T(8,128)S(1)}, f32[32,18,1,128]{3,0,2,1:T(8,128)S(1)}, u32[]{:S(2)}, u32[]{:S(2)}) collective-permute-start(f32[32,18,1,128]{3,0,2,1:T(8,128)S(1)} %get-tuple-element.15), channel_id=1, source_target_pairs={{0,2},{2,4},{4,6},{6,8},{8,10},{10,12},{12,14},{1,3},{3,5},{5,7},{... | collective-permute-start | bytes 884744 | tf_op jit(solution)/shard_map/ppermute | solution.py:14
  171.5 70.4 %copy-start.4 = (f32[64,32]{0,1:T(8,128)S(1)}, f32[64,32]{0,1:T(8,128)}, u32[]{:S(2)}) copy-start(f32[64,32]{0,1:T(8,128)} %param.11) | copy-start | bytes 24580
  (3 other events, 23.0 us)
Sparse Core Ops, SparseCore 0:
  164.8 63.8 all-gather.1
